TPU v7x, 32 devices: a whole 2x2x4 slice. The times are simulated.
32 devices in a mesh: tm: 2 (over core), lat: 16 (over z, y, x).
Axes of the slice: x: 2, y: 2, z: 4, core: 2. Of those that a mesh axis runs over, the one named last changes fastest.
Arguments:
- spectral_state: float32 [4, 16, 2, 16, 256], P('tm', 'lat'), may hold values from -6 to 6
- legendre: bfloat16 [16, 16, 16], P('lat'), may hold values from -1.5 to 1.5
- wave_slots: int32 [16], replicated, may hold values from 0 to 15, each once
- lat_order: int32 [16], replicated, may hold values from 0 to 15, each once
- quad_weights: float32 [16], replicated, may hold values from 0.2 to 1
- available: int32 [4, 8, 16, 256], P('tm', None, 'lat'), may hold values 0 or 1
- targets: float32 [4, 4, 8], P('tm'), may hold values from -6 to 6
- w_first: float32 [256, 384], replicated, may hold values from -0.375 to 0.375
- w_mid: float32 [384, 384], replicated, may hold values from -0.3125 to 0.3125
- w_last: float32 [384, 256], replicated, may hold values from -0.3125 to 0.3125
- norm_bias: float32 [2, 1024], replicated, may hold values from -0.3 to 0.3
- mean_first: float32 [256, 384], replicated, may hold values from -0.00061035156 to 0.00061035156
- mean_mid: float32 [384, 384], replicated, may hold values from -0.00061035156 to 0.00061035156
- mean_last: float32 [384, 256], replicated, may hold values from -0.00061035156 to 0.00061035156
- mean_bias: float32 [2, 1024], replicated, may hold values from -0.00061035156 to 0.00061035156
- square_first: float32 [256, 384], replicated, may hold values from 3e-10 to 3e-08
- square_mid: float32 [384, 384], replicated, may hold values from 3e-10 to 3e-08
- square_last: float32 [384, 256], replicated, may hold values from 3e-10 to 3e-08
- square_bias: float32 [2, 1024], replicated, may hold values from 3e-10 to 3e-08
Outputs:
- loss: float32 [], replicated
- grad_norm: float32 [], replicated
- master_first: float32 [256, 384], replicated
- master_mid: float32 [384, 384], replicated
- master_last: float32 [384, 256], replicated
- master_bias: float32 [2, 1024], replicated
- new_mean_first: float32 [256, 384], replicated
- new_mean_mid: float32 [384, 384], replicated
- new_mean_last: float32 [384, 256], replicated
- new_mean_bias: float32 [2, 1024], replicated
- new_square_first: float32 [256, 384], replicated
- new_square_mid: float32 [384, 384], replicated
- new_square_last: float32 [384, 256], replicated
- new_square_bias: float32 [2, 1024], replicated
- half_first: bfloat16 [256, 384], replicated
- half_mid: bfloat16 [384, 384], replicated
- half_last: bfloat16 [384, 256], replicated
- half_bias: bfloat16 [2, 1024], replicated
Inputs may be any that keep to these rules, and one draw needn't show every extreme that they name: `wave_slots`: each wavenumber 0 to 15 stands in one slot; slot j lies on the device of index j // 1 of lat. `lat_order`: each latitude stands in one grid row.
All inputs are finite; a program needn't handle non-finite values. No bound on the sum of `available` on one device may be relied on, other than what follows from the above.
Results may differ from a plain program's by a relative error of at most 0.0082.
Values may be sent and summed in bfloat16 or wider, within the bound.
No kernel may reach another device: no remote copies, remote signals or barrier semaphores. Data moves between devices by JAX's collectives and lax.ppermute only.
A program may use at most 128 MiB of HBM per device.

v0:
```python
from functools import partial
import math
import jax
import jax.numpy as jnp
from jax import lax
from jax.sharding import PartitionSpec as P

STEPS = 4
EPS_NORM = 1e-05
STEP_SCALE = 0.5
CLIP_NORM = 1.0
LEARN_RATE = 0.01
BETA_ONE = 0.9
BETA_TWO = 0.95
EPS_ADAM = 1e-08
DECAY = 0.1
HIGH = lax.Precision.HIGHEST


def wave_tables(wave_slots, lon_count):
    product = wave_slots[:, None] * jnp.arange(lon_count, dtype=jnp.int32)[None, :] % lon_count
    phase = product.astype(jnp.float32) * (2.0 * math.pi / lon_count)
    inverse = jnp.stack([jnp.cos(phase), -jnp.sin(phase)], axis=1)
    scale = jnp.where(wave_slots == 0, 1.0, 2.0).astype(jnp.float32) / lon_count
    return (inverse.astype(jnp.bfloat16), (inverse * scale[:, None, None]).astype(jnp.bfloat16))


def layer_spans(chans, hidden):
    gains = [(0, chans), (chans, hidden), (chans + hidden, hidden)]
    biases = [(0, hidden), (hidden, hidden), (2 * hidden, chans)]
    return list(zip(gains, biases))


def norm_gain(x, gain):
    centre = x - jnp.mean(x, axis=-1, keepdims=True)
    return centre * lax.rsqrt(jnp.mean(centre * centre, axis=-1, keepdims=True) + EPS_NORM) * gain


def corrector_forward(x, weights, norm_bias):
    spans = layer_spans(weights[0].shape[0], weights[0].shape[1])
    saved = []
    for k in range(3):
        (gstart, gwidth), (bstart, bwidth) = spans[k]
        h_low = norm_gain(x, 1.0 + norm_bias[0, gstart : gstart + gwidth]).astype(jnp.bfloat16)
        z_val = (
            jnp.dot(h_low, weights[k], preferred_element_type=jnp.float32)
            + norm_bias[1, bstart : bstart + bwidth]
        )
        saved.append((x, h_low, z_val))
        x = jax.nn.gelu(z_val, approximate=False) if k < 2 else z_val
    return (x, saved)


def corrector_backward(grad, saved, weights, norm_bias):
    spans = layer_spans(weights[0].shape[0], weights[0].shape[1])
    weight_grads = [None, None, None]
    gain_parts = [None, None, None]
    bias_parts = [None, None, None]
    for k in (2, 1, 0):
        (gstart, gwidth), (bstart, bwidth) = spans[k]
        x, h_low, z_val = saved[k]
        if k < 2:
            grad = jax.vjp(partial(jax.nn.gelu, approximate=False), z_val)[1](grad)[0]
        grad_low = grad.astype(jnp.bfloat16)
        weight_grads[k] = lax.dot_general(
            h_low, grad_low, (((0,), (0,)), ((), ())), preferred_element_type=jnp.float32
        )
        bias_parts[k] = jnp.sum(grad_low, axis=0, dtype=jnp.float32)
        back_h = lax.dot_general(
            grad_low, weights[k], (((1,), (1,)), ((), ())), preferred_element_type=jnp.float32
        )
        grad, gain_parts[k] = jax.vjp(norm_gain, x, 1.0 + norm_bias[0, gstart : gstart + gwidth])[
            1
        ](back_h)
    vector_grad = jnp.stack([jnp.concatenate(gain_parts), jnp.concatenate(bias_parts)])
    return (grad, (weight_grads[0], weight_grads[1], weight_grads[2], vector_grad))


def adamw(weight, mean, square, grad):
    mean_new = BETA_ONE * mean + (1.0 - BETA_ONE) * grad
    square_new = BETA_TWO * square + (1.0 - BETA_TWO) * grad * grad
    weight_new = weight - LEARN_RATE * (
        mean_new / (jnp.sqrt(square_new) + EPS_ADAM) + DECAY * weight
    )
    return (weight_new, mean_new, square_new)


def per_device(
    spectral_state,
    legendre,
    wave_slots,
    lat_order,
    quad_weights,
    available,
    targets,
    w_first,
    w_mid,
    w_last,
    norm_bias,
    mean_first,
    mean_mid,
    mean_last,
    mean_bias,
    square_first,
    square_mid,
    square_last,
    square_bias,
):
    tdev, wdev, _, degrees, chans = spectral_state.shape
    fields = available.shape[1]
    rows_dev = available.shape[2]
    lon_count = available.shape[3]
    levels = chans // fields
    lat_index = lax.axis_index("lat")
    slots = lax.dynamic_slice_in_dim(wave_slots, lat_index * wdev, wdev)
    finv, ffw = wave_tables(wave_slots, lon_count)
    keep = (jnp.arange(degrees, dtype=jnp.int32)[None, :] >= slots[:, None]).astype(jnp.bfloat16)
    plg = jnp.take(legendre, lat_order, axis=2) * keep[:, :, None]
    qrow = jnp.take(quad_weights, lat_order)
    qlocal = lax.dynamic_slice_in_dim(qrow, lat_index * rows_dev, rows_dev)
    colw = qlocal[None, None, :, None] * available.astype(jnp.float32)
    den_part = jnp.sum(colw, axis=(2, 3))
    params = (w_first, w_mid, w_last, norm_bias)
    weights = (
        w_first.astype(jnp.bfloat16),
        w_mid.astype(jnp.bfloat16),
        w_last.astype(jnp.bfloat16),
    )

    def legendre_sum(piece):
        return jnp.einsum("mnr,tmprc->tmpnc", plg, piece, preferred_element_type=jnp.float32)

    def fourier_sum(table, piece):
        return jnp.einsum("mpk,tmprc->trkc", table, piece, preferred_element_type=jnp.float32)

    def to_grid(state):
        sums = jnp.einsum(
            "mnr,tmpnc->tmprc", plg, state.astype(jnp.bfloat16), preferred_element_type=jnp.float32
        ).astype(jnp.bfloat16)
        return fourier_sum(
            finv, lax.all_to_all(sums, "lat", split_axis=3, concat_axis=1, tiled=True)
        )

    def column_pass(grid):
        out, saved = corrector_forward(grid.reshape(-1, chans), weights, norm_bias)
        return (out.reshape(grid.shape), saved)

    states = []
    nums = []
    den_total = den_part
    state = spectral_state
    for s in range(STEPS):
        states.append(state)
        grid = to_grid(state)
        out, saved = column_pass(grid)
        pred = grid + STEP_SCALE * out
        num_part = jnp.einsum(
            "tfrk,trkfl->tf",
            colw,
            pred.reshape(tdev, rows_dev, lon_count, fields, levels),
            precision=HIGH,
        )
        num_total, den_total = lax.psum((num_part, den_part), "lat")
        nums.append(num_total)
        tend = (out * qlocal[None, :, None, None]).astype(jnp.bfloat16)
        coeff = jnp.einsum("mpk,trkc->tmprc", ffw, tend, preferred_element_type=jnp.float32).astype(
            jnp.bfloat16
        )
        spec = legendre_sum(lax.all_to_all(coeff, "lat", split_axis=1, concat_axis=3, tiled=True))
        state = state + STEP_SCALE * spec
    num_all = jnp.stack(nums)
    bias = num_all / (levels * den_total[None]) - jnp.moveaxis(targets, 1, 0)
    loss = lax.psum(jnp.sum(bias * bias) / STEPS, "tm")
    grad_bias = 2.0 * bias / (STEPS * levels * den_total[None])
    totals = tuple((jnp.zeros_like(p) for p in params))
    back_state = None
    for s in reversed(range(STEPS)):
        grid = to_grid(states[s])
        out, saved = column_pass(grid)
        scaled = jnp.moveaxis(colw * grad_bias[s][:, :, None, None], 1, 3)
        back_pred = jnp.broadcast_to(scaled[..., None], scaled.shape + (levels,)).reshape(
            grid.shape
        )
        back_out = STEP_SCALE * back_pred
        if back_state is not None:
            back_spec = (STEP_SCALE * back_state).astype(jnp.bfloat16)
            back_coeff = jnp.einsum(
                "mnr,tmpnc->tmprc", plg, back_spec, preferred_element_type=jnp.float32
            ).astype(jnp.bfloat16)
            back_tend = fourier_sum(
                ffw, lax.all_to_all(back_coeff, "lat", split_axis=3, concat_axis=1, tiled=True)
            )
            back_out = back_out + qlocal[None, :, None, None] * back_tend
        back_in, grads = corrector_backward(back_out.reshape(-1, chans), saved, weights, norm_bias)
        totals = tuple((a + b for a, b in zip(totals, grads)))
        if s > 0:
            back_grid = (back_pred + back_in.reshape(grid.shape)).astype(jnp.bfloat16)
            back_sums = jnp.einsum(
                "mpk,trkc->tmprc", finv, back_grid, preferred_element_type=jnp.float32
            ).astype(jnp.bfloat16)
            back_low = legendre_sum(
                lax.all_to_all(back_sums, "lat", split_axis=1, concat_axis=3, tiled=True)
            )
            back_state = back_low if back_state is None else back_state + back_low
    means = (mean_first, mean_mid, mean_last, mean_bias)
    squares = (square_first, square_mid, square_last, square_bias)
    grads = lax.psum(totals, ("tm", "lat"))
    grad_norm = jnp.sqrt(sum((jnp.sum(g * g) for g in grads)))
    factor = CLIP_NORM / jnp.maximum(grad_norm, CLIP_NORM)
    results = [adamw(w, a, b, g * factor) for w, a, b, g in zip(params, means, squares, grads)]
    masters = [r[0] for r in results]
    new_means = [r[1] for r in results]
    new_squares = [r[2] for r in results]
    halves = [w.astype(jnp.bfloat16) for w in masters]
    return (
        loss,
        grad_norm,
        masters[0],
        masters[1],
        masters[2],
        masters[3],
        new_means[0],
        new_means[1],
        new_means[2],
        new_means[3],
        new_squares[0],
        new_squares[1],
        new_squares[2],
        new_squares[3],
        halves[0],
        halves[1],
        halves[2],
        halves[3],
    )


def solution(mesh):
    in_specs = (
        P("tm", "lat", None, None, None),
        P("lat", None, None),
        P(),
        P(),
        P(),
        P("tm", None, "lat", None),
        P("tm", None, None),
        P(),
        P(),
        P(),
        P(),
        P(),
        P(),
        P(),
        P(),
        P(),
        P(),
        P(),
        P(),
    )
    out_specs = (
        P(),
        P(),
        P(),
        P(),
        P(),
        P(),
        P(),
        P(),
        P(),
        P(),
        P(),
        P(),
        P(),
        P(),
        P(),
        P(),
        P(),
        P(),
    )
    return jax.shard_map(
        per_device, mesh=mesh, in_specs=in_specs, out_specs=out_specs, check_vma=False
    )
```

profile of v0, /device:TPU:0, one launch (start us, length us, event | category | flops | bytes accessed | tf_op | source)
XLA Modules:
  0.0 490.8 jit_solution(849199737556524078)
XLA Ops:
  11.4 8.3 %all-to-all-start = ((bf16[2,1,2,16,256]{4,2,0,1,3:T(2,128)(2,1)}), bf16[2,1,2,16,256]{4,2,0,1,3:T(2,128)(2,1)S(1)}, u32[]{:S(2)}, u32[]{:S(2)}) async-start(bf16[2,1,2,16,256]{4,2,0,1,3:T(2,128)(2,1)} %copy.194), calls=%async_computation | async-start | bytes 65536 | tf_op jit(solution)/shard_map/all_to_all | solution.py:141
  21.9 5.3 %all-to-all-done = bf16[2,1,2,16,256]{4,2,0,1,3:T(2,128)(2,1)S(1)} async-done(((bf16[2,1,2,16,256]{4,2,0,1,3:T(2,128)(2,1)}), bf16[2,1,2,16,256]{4,2,0,1,3:T(2,128)(2,1)S(1)}, u32[]{:S(2)}, u32[]{:S(2)}) %all-to-all-start) | async-done | bytes 32800 | tf_op jit(solution)/shard_map/all_to_all | solution.py:141
  37.8 10.0 %all_to_all.215 = bf16[2,16,2,1,256]{4,2,0,3,1:T(2,128)(2,1)S(1)} all-to-all(bf16[2,16,2,1,256]{4,2,0,3,1:T(2,128)(2,1)S(1)} %copy.198), channel_id=1, replica_groups=mesh['tm'=2,'lat'=16] {'lat'}, dimensions={1} | all-to-all | bytes 65536 | tf_op jit(solution)/shard_map/all_to_all | solution.py:169
  48.2 10.1 %all_to_all.216 = bf16[2,1,2,16,256]{4,2,0,1,3:T(2,128)(2,1)S(1)} all-to-all(bf16[2,1,2,16,256]{4,2,0,1,3:T(2,128)(2,1)S(1)} %copy.202), channel_id=1, replica_groups=mesh['tm'=2,'lat'=16] {'lat'}, dimensions={3} | all-to-all | bytes 65536 | tf_op jit(solution)/shard_map/all_to_all | solution.py:141
  70.5 10.0 %all_to_all.217 = bf16[2,16,2,1,256]{4,2,0,3,1:T(2,128)(2,1)S(1)} all-to-all(bf16[2,16,2,1,256]{4,2,0,3,1:T(2,128)(2,1)S(1)} %copy.206), channel_id=1, replica_groups=mesh['tm'=2,'lat'=16] {'lat'}, dimensions={1} | all-to-all | bytes 65536 | tf_op jit(solution)/shard_map/all_to_all | solution.py:169
  80.8 10.0 %all_to_all.218 = bf16[2,1,2,16,256]{4,2,0,1,3:T(2,128)(2,1)S(1)} all-to-all(bf16[2,1,2,16,256]{4,2,0,1,3:T(2,128)(2,1)S(1)} %copy.209), channel_id=1, replica_groups=mesh['tm'=2,'lat'=16] {'lat'}, dimensions={3} | all-to-all | bytes 65536 | tf_op jit(solution)/shard_map/all_to_all | solution.py:141
  102.1 10.0 %all_to_all.219 = bf16[2,16,2,1,256]{4,2,0,3,1:T(2,128)(2,1)S(1)} all-to-all(bf16[2,16,2,1,256]{4,2,0,3,1:T(2,128)(2,1)S(1)} %copy.213), channel_id=1, replica_groups=mesh['tm'=2,'lat'=16] {'lat'}, dimensions={1} | all-to-all | bytes 65536 | tf_op jit(solution)/shard_map/all_to_all | solution.py:169
  113.0 3.8 all-to-all-start.6
  150.4 42.5 %all-reduce.1 = (f32[1,2,8]{2,1,0:T(2,128)S(1)}, f32[1,2,8]{2,1,0:T(2,128)S(1)}, f32[1,2,8]{2,1,0:T(2,128)S(1)}, f32[1,2,8]{2,1,0:T(2,128)S(1)}, f32[2,8]{1,0:T(2,128)S(1)}) all-reduce(f32[1,2,8]{2,1,0:T(2,128)S(1)} %bitcast.673, f32[1,2,8]{2,1,0:T(2,128)S(1)} %bitcast.674, ...), channel_id=1, replica_groups=mesh['tm'=2,'lat'=16] {'lat'}, use_global_device_ids=true, to_apply=%region_31.32 | all-reduce | flops 80 | bytes 640 | tf_op jit(solution)/shard_map/psum | solution.py:163
  210.8 3.4 psum.75
  230.8 3.6 all-to-all-start.7
  235.2 6.7 %all-to-all-done.7 = bf16[2,16,2,1,256]{4,2,0,3,1:T(2,128)(2,1)S(1)} async-done(((bf16[2,16,2,1,256]{4,2,0,3,1:T(2,128)(2,1)}), bf16[2,16,2,1,256]{4,2,0,3,1:T(2,128)(2,1)S(1)}, u32[]{:S(2)}, u32[]{:S(2)}) %all-to-all-start.7) | async-done | bytes 32800 | tf_op jit(solution)/shard_map/all_to_all | solution.py:202
  242.8 3.5 all-to-all-start.8
  247.0 6.6 %all-to-all-done.8 = bf16[2,1,2,16,256]{4,2,0,1,3:T(2,128)(2,1)S(1)} async-done(((bf16[2,1,2,16,256]{4,2,0,1,3:T(2,128)(2,1)}), bf16[2,1,2,16,256]{4,2,0,1,3:T(2,128)(2,1)S(1)}, u32[]{:S(2)}, u32[]{:S(2)}) %all-to-all-start.8) | async-done | bytes 32800 | tf_op jit(solution)/shard_map/all_to_all | solution.py:191
  268.9 3.5 all-to-all-start.9
  272.4 7.4 %all-to-all-done.9 = bf16[2,16,2,1,256]{4,2,0,3,1:T(2,128)(2,1)S(1)} async-done(((bf16[2,16,2,1,256]{4,2,0,3,1:T(2,128)(2,1)}), bf16[2,16,2,1,256]{4,2,0,3,1:T(2,128)(2,1)S(1)}, u32[]{:S(2)}, u32[]{:S(2)}) %all-to-all-start.9) | async-done | bytes 32800 | tf_op jit(solution)/shard_map/all_to_all | solution.py:202
  280.7 3.5 all-to-all-start.10
  284.2 7.4 %all-to-all-done.10 = bf16[2,1,2,16,256]{4,2,0,1,3:T(2,128)(2,1)S(1)} async-done(((bf16[2,1,2,16,256]{4,2,0,1,3:T(2,128)(2,1)}), bf16[2,1,2,16,256]{4,2,0,1,3:T(2,128)(2,1)S(1)}, u32[]{:S(2)}, u32[]{:S(2)}) %all-to-all-start.10) | async-done | bytes 32800 | tf_op jit(solution)/shard_map/all_to_all | solution.py:191
  305.2 3.7 all-to-all-start.11
  311.0 5.2 %all-to-all-done.11 = bf16[2,16,2,1,256]{4,2,0,3,1:T(2,128)(2,1)S(1)} async-done(((bf16[2,16,2,1,256]{4,2,0,3,1:T(2,128)(2,1)}), bf16[2,16,2,1,256]{4,2,0,3,1:T(2,128)(2,1)S(1)}, u32[]{:S(2)}, u32[]{:S(2)}) %all-to-all-start.11) | async-done | bytes 32800 | tf_op jit(solution)/shard_map/all_to_all | solution.py:202
  317.2 3.5 all-to-all-start.12
  320.8 7.3 %all-to-all-done.12 = bf16[2,1,2,16,256]{4,2,0,1,3:T(2,128)(2,1)S(1)} async-done(((bf16[2,1,2,16,256]{4,2,0,1,3:T(2,128)(2,1)}), bf16[2,1,2,16,256]{4,2,0,1,3:T(2,128)(2,1)S(1)}, u32[]{:S(2)}, u32[]{:S(2)}) %all-to-all-start.12) | async-done | bytes 32800 | tf_op jit(solution)/shard_map/all_to_all | solution.py:191
  339.6 38.5 %psum.79 = f32[2,1024]{1,0:T(2,128)S(1)} all-reduce(f32[2,1024]{1,0:T(2,128)S(1)} %fusion.164), channel_id=1, replica_groups=mesh['tm'=2,'lat'=16] {'tm','lat'}, use_global_device_ids=true, to_apply=%region_88.89 | all-reduce | flops 2048 | bytes 16384 | tf_op jit(solution)/shard_map/psum | solution.py:207
  378.8 90.0 %all-reduce.4.cloned.1.call-done = (f32[256,384]{1,0:T(8,128)}, f32[384,384]{1,0:T(8,128)}, f32[384,256]{1,0:T(8,128)}) async-done(((f32[256,384]{1,0:T(8,128)}, f32[384,384]{1,0:T(8,128)}, f32[384,256]{1,0:T(8,128)}), (f32[256,384]{1,0:T(8,128)}, f32[384,384]{1,0:T(8,128)}, f32[384,256]{1,0:T(8,128)})) %all-reduce.4.cloned.1.call-update) | async-done | bytes 1376272 | tf_op jit(solution)/shard_map/psum | solution.py:207
  (536 shorter events, 166.8 us)
Async XLA Ops:
  9.2 11.4 %copy-start.37 = (f32[256,384]{1,0:T(8,128)S(1)}, f32[256,384]{1,0:T(8,128)}, u32[]{:S(2)}) copy-start(f32[256,384]{1,0:T(8,128)} %param.26) | copy-start | bytes 1179652
  10.6 9.1 %copy-start.91 = (f32[2,1024]{1,0:T(2,128)S(1)}, f32[2,1024]{1,0:T(2,128)}, u32[]{:S(2)}) copy-start(f32[2,1024]{1,0:T(2,128)} %param.29) | copy-start | bytes 24580
  10.8 9.9 %copy-start.39 = (f32[384,256]{1,0:T(8,128)S(1)}, f32[384,256]{1,0:T(8,128)}, u32[]{:S(2)}) copy-start(f32[384,256]{1,0:T(8,128)} %param.28) | copy-start | bytes 1179652
  11.4 15.8 %all-to-all-start = ((bf16[2,1,2,16,256]{4,2,0,1,3:T(2,128)(2,1)}), bf16[2,1,2,16,256]{4,2,0,1,3:T(2,128)(2,1)S(1)}, u32[]{:S(2)}, u32[]{:S(2)}) async-start(bf16[2,1,2,16,256]{4,2,0,1,3:T(2,128)(2,1)} %copy.194), calls=%async_computation | async-start | bytes 65536 | tf_op jit(solution)/shard_map/all_to_all | solution.py:141
  19.8 73.5 %copy-start.139 = (f32[384]{0:T(512)}, f32[384]{0:T(512)S(1)}, u32[]{:S(2)}) copy-start(f32[384]{0:T(512)S(1)} %get-tuple-element.47) | copy-start | bytes 4612
  19.8 76.8 %copy-start.137 = (f32[384]{0:T(512)}, f32[384]{0:T(512)S(1)}, u32[]{:S(2)}) copy-start(f32[384]{0:T(512)S(1)} %get-tuple-element.45) | copy-start | bytes 4612
  20.6 72.7 %copy-start.24 = (bf16[256,384]{1,0:T(8,128)(2,1)}, bf16[256,384]{1,0:T(8,128)(2,1)S(1)}, u32[]{:S(2)}) copy-start(bf16[256,384]{1,0:T(8,128)(2,1)S(1)} %convert_element_type.413) | copy-start | bytes 589828
  21.8 74.9 %copy-start.21 = (bf16[384,384]{1,0:T(8,128)(2,1)}, bf16[384,384]{1,0:T(8,128)(2,1)S(1)}, u32[]{:S(2)}) copy-start(bf16[384,384]{1,0:T(8,128)(2,1)S(1)} %convert_element_type.415) | copy-start | bytes 884740
  113.0 19.9 %all-to-all-start.6 = ((bf16[2,1,2,16,256]{4,2,0,1,3:T(2,128)(2,1)}), bf16[2,1,2,16,256]{4,2,0,1,3:T(2,128)(2,1)S(1)}, u32[]{:S(2)}, u32[]{:S(2)}) async-start(bf16[2,1,2,16,256]{4,2,0,1,3:T(2,128)(2,1)} %copy.216), calls=%async_computation.6 | async-start | bytes 65536 | tf_op jit(solution)/shard_map/all_to_all | solution.py:141
  133.3 71.8 %copy-start.87 = (f32[1,2,2,128]{3,1,2,0:T(2,128)}, f32[1,2,2,128]{3,1,2,0:T(2,128)S(1)}, u32[]{:S(2)}) copy-start(f32[1,2,2,128]{3,1,2,0:T(2,128)S(1)} %copy.333) | copy-start | bytes 6148
  135.0 70.1 %copy-start.89 = (f32[512]{0:T(512)}, f32[512]{0:T(512)S(1)}, u32[]{:S(2)}) copy-start(f32[512]{0:T(512)S(1)} %rsqrt.155) | copy-start | bytes 6148
  208.6 5.5 %copy-start.136 = (f32[2,8]{1,0:T(2,128)S(1)}, f32[2,8]{1,0:T(2,128)}, u32[]{:S(2)}) copy-start(f32[2,8]{1,0:T(2,128)} %get-tuple-element.143) | copy-start | bytes 196
  230.8 11.0 %all-to-all-start.7 = ((bf16[2,16,2,1,256]{4,2,0,3,1:T(2,128)(2,1)}), bf16[2,16,2,1,256]{4,2,0,3,1:T(2,128)(2,1)S(1)}, u32[]{:S(2)}, u32[]{:S(2)}) async-start(bf16[2,16,2,1,256]{4,2,0,3,1:T(2,128)(2,1)} %copy.228), calls=%async_computation.7 | async-start | bytes 65536 | tf_op jit(solution)/shard_map/all_to_all | solution.py:202
  242.8 10.9 %all-to-all-start.8 = ((bf16[2,1,2,16,256]{4,2,0,1,3:T(2,128)(2,1)}), bf16[2,1,2,16,256]{4,2,0,1,3:T(2,128)(2,1)S(1)}, u32[]{:S(2)}, u32[]{:S(2)}) async-start(bf16[2,1,2,16,256]{4,2,0,1,3:T(2,128)(2,1)} %copy.231), calls=%async_computation.8 | async-start | bytes 65536 | tf_op jit(solution)/shard_map/all_to_all | solution.py:191
  268.0 23.6 %copy-start.36 = (f32[2,1,256,256]{3,2,0,1:T(8,128)S(1)}, f32[2,1,256,256]{3,2,0,1:T(8,128)}, u32[]{:S(2)}) copy-start(f32[2,1,256,256]{3,2,0,1:T(8,128)} %copy.243) | copy-start | bytes 1572868
  268.9 10.9 %all-to-all-start.9 = ((bf16[2,16,2,1,256]{4,2,0,3,1:T(2,128)(2,1)}), bf16[2,16,2,1,256]{4,2,0,3,1:T(2,128)(2,1)S(1)}, u32[]{:S(2)}, u32[]{:S(2)}) async-start(bf16[2,16,2,1,256]{4,2,0,3,1:T(2,128)(2,1)} %copy.238), calls=%async_computation.9 | async-start | bytes 65536 | tf_op jit(solution)/shard_map/all_to_all | solution.py:202
  280.7 10.9 %all-to-all-start.10 = ((bf16[2,1,2,16,256]{4,2,0,1,3:T(2,128)(2,1)}), bf16[2,1,2,16,256]{4,2,0,1,3:T(2,128)(2,1)S(1)}, u32[]{:S(2)}, u32[]{:S(2)}) async-start(bf16[2,1,2,16,256]{4,2,0,1,3:T(2,128)(2,1)} %copy.241), calls=%async_computation.10 | async-start | bytes 65536 | tf_op jit(solution)/shard_map/all_to_all | solution.py:191
  305.2 11.0 %all-to-all-start.11 = ((bf16[2,16,2,1,256]{4,2,0,3,1:T(2,128)(2,1)}), bf16[2,16,2,1,256]{4,2,0,3,1:T(2,128)(2,1)S(1)}, u32[]{:S(2)}, u32[]{:S(2)}) async-start(bf16[2,16,2,1,256]{4,2,0,3,1:T(2,128)(2,1)} %copy.248), calls=%async_computation.11 | async-start | bytes 65536 | tf_op jit(solution)/shard_map/all_to_all | solution.py:202
  308.9 19.2 %copy-start.35 = (f32[2,1,256,256]{3,2,0,1:T(8,128)S(1)}, f32[2,1,256,256]{3,2,0,1:T(8,128)}, u32[]{:S(2)}) copy-start(f32[2,1,256,256]{3,2,0,1:T(8,128)} %copy.253) | copy-start | bytes 1572868
  317.2 10.9 %all-to-all-start.12 = ((bf16[2,1,2,16,256]{4,2,0,1,3:T(2,128)(2,1)}), bf16[2,1,2,16,256]{4,2,0,1,3:T(2,128)(2,1)S(1)}, u32[]{:S(2)}, u32[]{:S(2)}) async-start(bf16[2,1,2,16,256]{4,2,0,1,3:T(2,128)(2,1)} %copy.251), calls=%async_computation.12 | async-start | bytes 65536 | tf_op jit(solution)/shard_map/all_to_all | solution.py:191
  320.7 148.0 %all-reduce.4.cloned.1.call-start = ((), (), s32[]{:S(2)}) async-start(), calls=%async_computation.13 | async-start | bytes 2752512 | tf_op jit(solution)/shard_map/psum | solution.py:207
  339.2 137.3 %copy-start.72 = (f32[256,384]{1,0:T(8,128)S(1)}, f32[256,384]{1,0:T(8,128)}, u32[]{:S(2)}) copy-start(f32[256,384]{1,0:T(8,128)} %param.30) | copy-start | bytes 1179652
  468.7 7.7 %copy-start.71 = (f32[256,384]{1,0:T(8,128)S(1)}, f32[256,384]{1,0:T(8,128)}, u32[]{:S(2)}) copy-start(f32[256,384]{1,0:T(8,128)} %param.34) | copy-start | bytes 1179652
  470.5 6.0 %copy-start.38 = (f32[256,384]{1,0:T(8,128)S(1)}, f32[256,384]{1,0:T(8,128)}, u32[]{:S(2)}) copy-start(f32[256,384]{1,0:T(8,128)} %param.26) | copy-start | bytes 1179652
  (128 other events, 199.3 us)
Sparse Core Ops, SparseCore 0:
  339.3 129.3 all-reduce.3
where the time goes:
time: 499 us; the launch traced here: 491 us
  waiting for transfers between devices  136 us (27%)
  blocking collectives  134 us (27%)
  matrix products  61.3 us (12%)
  local copies, waits for them, and re-layouts  61.2 us (12%)
  other arithmetic  44.3 us (9%)
  starting transfers between devices  33.5 us (7%)
  between operations  20.2 us (4%)
    psum x1, waiting for transfers between devices, per_device(): grads = lax.psum(totals, ('tm', 'lat'))  90 us
    psum x1, blocking collectives, per_device(): num_total, den_total = lax.psum((num_part, den_part), 'lat')  42.5 us
    psum x1, blocking collectives, per_device(): grads = lax.psum(totals, ('tm', 'lat'))  38.5 us
    dot_general x12, matrix products, corrector_forward(): jnp.dot(h_low, weights[k], preferred_element_type=jnp.float32)  31.7 us
    all_to_all x3, blocking collectives, per_device(): lax.all_to_all(coeff, 'lat', split_axis=1, concat_axis=3, tiled=True)  29.9 us
    unnamed x297, local copies, waits for them, and re-layouts  29.6 us
    all_to_all x3, waiting for transfers between devices, per_device(): lax.all_to_all(back_coeff, 'lat', split_axis=3, concat_axis=1, tiled=True)  21.3 us
    all_to_all x2, blocking collectives, to_grid(): lax.all_to_all(sums, 'lat', split_axis=3, concat_axis=1, tiled=True)  20.1 us
  transfers between devices with their start and end apart: 9, of which 8 were waited for; matrix products, arithmetic and copies ran while one was open for 4% of the time, Pallas kernels for 0%

commit v1 on v0

--- a/solution.py
+++ b/solution.py
@@ -15,6 +15,13 @@
 EPS_ADAM = 1e-08
 DECAY = 0.1
 HIGH = lax.Precision.HIGHEST
+
+
+def exchange_blocks(block, name, split, join):
+    peers = lax.axis_size(name)
+    pieces = jnp.stack(jnp.split(block, peers, axis=split), axis=0)
+    pieces = lax.all_to_all(pieces, name, split_axis=0, concat_axis=0)
+    return jnp.concatenate(pieces, axis=join)
 
 
 def wave_tables(wave_slots, lon_count):
@@ -137,9 +144,7 @@
         sums = jnp.einsum(
             "mnr,tmpnc->tmprc", plg, state.astype(jnp.bfloat16), preferred_element_type=jnp.float32
         ).astype(jnp.bfloat16)
-        return fourier_sum(
-            finv, lax.all_to_all(sums, "lat", split_axis=3, concat_axis=1, tiled=True)
-        )
+        return fourier_sum(finv, exchange_blocks(sums, "lat", 3, 1))
 
     def column_pass(grid):
         out, saved = corrector_forward(grid.reshape(-1, chans), weights, norm_bias)

time: 499 us -> 517 us (1.036)
  local copies, waits for them, and re-layouts: 61.2 us -> 80.3 us
    unnamed x297 -> x383, local copies, waits for them, and re-layouts: 29.6 us -> 50.5 us
where the time goes in v1:
time: 517 us; the launch traced here: 508 us
  blocking collectives  135 us (26%)
  waiting for transfers between devices  131 us (25%)
  local copies, waits for them, and re-layouts  80.3 us (16%)
  matrix products  60.9 us (12%)
  other arithmetic  47.8 us (9%)
  starting transfers between devices  33.2 us (6%)
  between operations  20.4 us (4%)
    psum x1, waiting for transfers between devices, per_device(): grads = lax.psum(totals, ('tm', 'lat'))  88.4 us
    unnamed x383, local copies, waits for them, and re-layouts  50.5 us
    psum x1, blocking collectives, per_device(): num_total, den_total = lax.psum((num_part, den_part), 'lat')  42.5 us
    psum x1, blocking collectives, per_device(): grads = lax.psum(totals, ('tm', 'lat'))  38.6 us
    dot_general x12, matrix products, corrector_forward(): jnp.dot(h_low, weights[k], preferred_element_type=jnp.float32)  31.7 us
    all_to_all x3, blocking collectives, per_device(): lax.all_to_all(coeff, 'lat', split_axis=1, concat_axis=3, tiled=True)  30.1 us
    all_to_all x2, blocking collectives, exchange_blocks(): pieces = lax.all_to_all(pieces, name, split_axis=0, concat_axis=0)  20.1 us
    all_to_all x3, waiting for transfers between devices, per_device(): lax.all_to_all(back_sums, 'lat', split_axis=1, concat_axis=3, tiled=True)  18.8 us
  transfers between devices with their start and end apart: 9, of which 8 were waited for; matrix products, arithmetic and copies ran while one was open for 4% of the time, Pallas kernels for 0%

profile of v1, /device:TPU:0, one launch (start us, length us, event | category | flops | bytes accessed | tf_op | source)
XLA Modules:
  0.0 508.5 jit_solution(5362676561432040328)
XLA Ops:
  20.1 8.3 %all-to-all-start = ((bf16[16,2,1,2,1,256]{5,3,1,4,2,0:T(2,128)(2,1)}), bf16[16,2,1,2,1,256]{5,3,1,4,2,0:T(2,128)(2,1)S(1)}, u32[]{:S(2)}, u32[]{:S(2)}) async-start(bf16[16,2,1,2,1,256]{5,3,1,4,2,0:T(2,128)(2,1)} %constant_dynamic-update-slice_fusion), calls=%async_computation | async-start | bytes 65536 | tf_op jit(solution)/shard_map/all_to_all | solution.py:23
  30.6 5.3 %all-to-all-done = bf16[16,2,1,2,1,256]{5,3,1,4,2,0:T(2,128)(2,1)S(1)} async-done(((bf16[16,2,1,2,1,256]{5,3,1,4,2,0:T(2,128)(2,1)}), bf16[16,2,1,2,1,256]{5,3,1,4,2,0:T(2,128)(2,1)S(1)}, u32[]{:S(2)}, u32[]{:S(2)}) %all-to-all-start) | async-done | bytes 32800 | tf_op jit(solution)/shard_map/all_to_all | solution.py:23
  47.1 10.0 %all_to_all.159 = bf16[2,16,2,1,256]{4,2,0,3,1:T(2,128)(2,1)S(1)} all-to-all(bf16[2,16,2,1,256]{4,2,0,3,1:T(2,128)(2,1)S(1)} %copy.1491), channel_id=1, replica_groups=mesh['tm'=2,'lat'=16] {'lat'}, dimensions={1} | all-to-all | bytes 65536 | tf_op jit(solution)/shard_map/all_to_all | solution.py:174
  57.7 10.1 %all_to_all.160 = bf16[16,2,1,2,1,256]{5,3,1,4,2,0:T(2,128)(2,1)S(1)} all-to-all(bf16[16,2,1,2,1,256]{5,3,1,4,2,0:T(2,128)(2,1)S(1)} %constant_dynamic-update-slice_fusion.16), channel_id=1, replica_groups=mesh['tm'=2,'lat'=16] {'lat'}, dimensions={0} | all-to-all | bytes 65536 | tf_op jit(solution)/shard_map/all_to_all | solution.py:23
  80.0 10.0 %all_to_all.161 = bf16[2,16,2,1,256]{4,2,0,3,1:T(2,128)(2,1)S(1)} all-to-all(bf16[2,16,2,1,256]{4,2,0,3,1:T(2,128)(2,1)S(1)} %copy.1498), channel_id=1, replica_groups=mesh['tm'=2,'lat'=16] {'lat'}, dimensions={1} | all-to-all | bytes 65536 | tf_op jit(solution)/shard_map/all_to_all | solution.py:174
  90.6 10.0 %all_to_all.162 = bf16[16,2,1,2,1,256]{5,3,1,4,2,0:T(2,128)(2,1)S(1)} all-to-all(bf16[16,2,1,2,1,256]{5,3,1,4,2,0:T(2,128)(2,1)S(1)} %constant_dynamic-update-slice_fusion.32), channel_id=1, replica_groups=mesh['tm'=2,'lat'=16] {'lat'}, dimensions={0} | all-to-all | bytes 65536 | tf_op jit(solution)/shard_map/all_to_all | solution.py:23
  113.0 10.2 %all_to_all.163 = bf16[2,16,2,1,256]{4,2,0,3,1:T(2,128)(2,1)S(1)} all-to-all(bf16[2,16,2,1,256]{4,2,0,3,1:T(2,128)(2,1)S(1)} %copy.1504), channel_id=1, replica_groups=mesh['tm'=2,'lat'=16] {'lat'}, dimensions={1} | all-to-all | bytes 65536 | tf_op jit(solution)/shard_map/all_to_all | solution.py:174
  132.8 3.6 all-to-all-start.6
  170.0 42.5 %all-reduce.1 = (f32[1,2,8]{2,1,0:T(2,128)S(1)}, f32[1,2,8]{2,1,0:T(2,128)S(1)}, f32[1,2,8]{2,1,0:T(2,128)S(1)}, f32[1,2,8]{2,1,0:T(2,128)S(1)}, f32[2,8]{1,0:T(2,128)S(1)}) all-reduce(f32[1,2,8]{2,1,0:T(2,128)S(1)} %bitcast.793, f32[1,2,8]{2,1,0:T(2,128)S(1)} %bitcast.794, ...), channel_id=1, replica_groups=mesh['tm'=2,'lat'=16] {'lat'}, use_global_device_ids=true, to_apply=%region_31.32 | all-reduce | flops 80 | bytes 640 | tf_op jit(solution)/shard_map/psum | solution.py:168
  228.3 3.4 psum.75
  245.8 3.5 all-to-all-start.7
  250.0 6.7 %all-to-all-done.7 = bf16[2,16,2,1,256]{4,2,0,3,1:T(2,128)(2,1)S(1)} async-done(((bf16[2,16,2,1,256]{4,2,0,3,1:T(2,128)(2,1)}), bf16[2,16,2,1,256]{4,2,0,3,1:T(2,128)(2,1)S(1)}, u32[]{:S(2)}, u32[]{:S(2)}) %all-to-all-start.7) | async-done | bytes 32800 | tf_op jit(solution)/shard_map/all_to_all | solution.py:207
  257.7 3.5 all-to-all-start.8
  262.5 6.1 %all-to-all-done.8 = bf16[2,1,2,16,256]{4,2,0,1,3:T(2,128)(2,1)S(1)} async-done(((bf16[2,1,2,16,256]{4,2,0,1,3:T(2,128)(2,1)}), bf16[2,1,2,16,256]{4,2,0,1,3:T(2,128)(2,1)S(1)}, u32[]{:S(2)}, u32[]{:S(2)}) %all-to-all-start.8) | async-done | bytes 32800 | tf_op jit(solution)/shard_map/all_to_all | solution.py:196
  283.7 3.5 all-to-all-start.9
  287.9 6.8 %all-to-all-done.9 = bf16[2,16,2,1,256]{4,2,0,3,1:T(2,128)(2,1)S(1)} async-done(((bf16[2,16,2,1,256]{4,2,0,3,1:T(2,128)(2,1)}), bf16[2,16,2,1,256]{4,2,0,3,1:T(2,128)(2,1)S(1)}, u32[]{:S(2)}, u32[]{:S(2)}) %all-to-all-start.9) | async-done | bytes 32800 | tf_op jit(solution)/shard_map/all_to_all | solution.py:207
  295.6 3.5 all-to-all-start.10
  300.4 6.1 %all-to-all-done.10 = bf16[2,1,2,16,256]{4,2,0,1,3:T(2,128)(2,1)S(1)} async-done(((bf16[2,1,2,16,256]{4,2,0,1,3:T(2,128)(2,1)}), bf16[2,1,2,16,256]{4,2,0,1,3:T(2,128)(2,1)S(1)}, u32[]{:S(2)}, u32[]{:S(2)}) %all-to-all-start.10) | async-done | bytes 32800 | tf_op jit(solution)/shard_map/all_to_all | solution.py:196
  322.2 3.7 all-to-all-start.11
  328.0 5.2 %all-to-all-done.11 = bf16[2,16,2,1,256]{4,2,0,3,1:T(2,128)(2,1)S(1)} async-done(((bf16[2,16,2,1,256]{4,2,0,3,1:T(2,128)(2,1)}), bf16[2,16,2,1,256]{4,2,0,3,1:T(2,128)(2,1)S(1)}, u32[]{:S(2)}, u32[]{:S(2)}) %all-to-all-start.11) | async-done | bytes 32800 | tf_op jit(solution)/shard_map/all_to_all | solution.py:207
  334.2 3.5 all-to-all-start.12
  338.5 6.6 %all-to-all-done.12 = bf16[2,1,2,16,256]{4,2,0,1,3:T(2,128)(2,1)S(1)} async-done(((bf16[2,1,2,16,256]{4,2,0,1,3:T(2,128)(2,1)}), bf16[2,1,2,16,256]{4,2,0,1,3:T(2,128)(2,1)S(1)}, u32[]{:S(2)}, u32[]{:S(2)}) %all-to-all-start.12) | async-done | bytes 32800 | tf_op jit(solution)/shard_map/all_to_all | solution.py:196
  358.8 38.6 %psum.79 = f32[2,1024]{1,0:T(2,128)S(1)} all-reduce(f32[2,1024]{1,0:T(2,128)S(1)} %fusion.164), channel_id=1, replica_groups=mesh['tm'=2,'lat'=16] {'tm','lat'}, use_global_device_ids=true, to_apply=%region_88.89 | all-reduce | flops 2048 | bytes 16384 | tf_op jit(solution)/shard_map/psum | solution.py:212
  397.9 88.4 %all-reduce.4.cloned.1.call-done = (f32[256,384]{1,0:T(8,128)}, f32[384,384]{1,0:T(8,128)}, f32[384,256]{1,0:T(8,128)}) async-done(((f32[256,384]{1,0:T(8,128)}, f32[384,384]{1,0:T(8,128)}, f32[384,256]{1,0:T(8,128)}), (f32[256,384]{1,0:T(8,128)}, f32[384,384]{1,0:T(8,128)}, f32[384,256]{1,0:T(8,128)})) %all-reduce.4.cloned.1.call-update) | async-done | bytes 1376272 | tf_op jit(solution)/shard_map/psum | solution.py:212
  (626 shorter events, 189.0 us)
Async XLA Ops:
  9.8 19.4 %copy-start.39 = (f32[256,384]{1,0:T(8,128)S(1)}, f32[256,384]{1,0:T(8,128)}, u32[]{:S(2)}) copy-start(f32[256,384]{1,0:T(8,128)} %param.26) | copy-start | bytes 1179652
  14.3 14.2 %copy-start.102 = (f32[2,1024]{1,0:T(2,128)S(1)}, f32[2,1024]{1,0:T(2,128)}, u32[]{:S(2)}) copy-start(f32[2,1024]{1,0:T(2,128)} %param.29) | copy-start | bytes 24580
  14.9 14.4 %copy-start.41 = (f32[384,256]{1,0:T(8,128)S(1)}, f32[384,256]{1,0:T(8,128)}, u32[]{:S(2)}) copy-start(f32[384,256]{1,0:T(8,128)} %param.28) | copy-start | bytes 1179652
  20.1 15.8 %all-to-all-start = ((bf16[16,2,1,2,1,256]{5,3,1,4,2,0:T(2,128)(2,1)}), bf16[16,2,1,2,1,256]{5,3,1,4,2,0:T(2,128)(2,1)S(1)}, u32[]{:S(2)}, u32[]{:S(2)}) async-start(bf16[16,2,1,2,1,256]{5,3,1,4,2,0:T(2,128)(2,1)} %constant_dynamic-update-slice_fusion), calls=%async_computation | async-start | bytes 65536 | tf_op jit(solution)/shard_map/all_to_all | solution.py:23
  28.5 41.3 %copy-start.151 = (f32[384]{0:T(512)}, f32[384]{0:T(512)S(1)}, u32[]{:S(2)}) copy-start(f32[384]{0:T(512)S(1)} %get-tuple-element.47) | copy-start | bytes 4612
  28.5 44.8 %copy-start.149 = (f32[384]{0:T(512)}, f32[384]{0:T(512)S(1)}, u32[]{:S(2)}) copy-start(f32[384]{0:T(512)S(1)} %get-tuple-element.45) | copy-start | bytes 4612
  29.3 73.8 %copy-start.24 = (bf16[256,384]{1,0:T(8,128)(2,1)}, bf16[256,384]{1,0:T(8,128)(2,1)S(1)}, u32[]{:S(2)}) copy-start(bf16[256,384]{1,0:T(8,128)(2,1)S(1)} %convert_element_type.413) | copy-start | bytes 589828
  30.5 76.4 %copy-start.21 = (bf16[384,384]{1,0:T(8,128)(2,1)}, bf16[384,384]{1,0:T(8,128)(2,1)S(1)}, u32[]{:S(2)}) copy-start(bf16[384,384]{1,0:T(8,128)(2,1)S(1)} %convert_element_type.415) | copy-start | bytes 884740
  132.8 19.7 %all-to-all-start.6 = ((bf16[16,2,1,2,1,256]{5,3,1,4,2,0:T(2,128)(2,1)}), bf16[16,2,1,2,1,256]{5,3,1,4,2,0:T(2,128)(2,1)S(1)}, u32[]{:S(2)}, u32[]{:S(2)}) async-start(bf16[16,2,1,2,1,256]{5,3,1,4,2,0:T(2,128)(2,1)} %constant_dynamic-update-slice_fusion.48), calls=%async_computation.6 | async-start | bytes 65536 | tf_op jit(solution)/shard_map/all_to_all | solution.py:23
  243.9 5.5 %copy-start.135 = (f32[384]{0:T(512)S(1)}, f32[384]{0:T(512)}, u32[]{:S(2)}) copy-start(f32[384]{0:T(512)} %get-tuple-element.86) | copy-start | bytes 4612
  243.9 5.5 %copy-start.139 = (f32[384]{0:T(512)S(1)}, f32[384]{0:T(512)}, u32[]{:S(2)}) copy-start(f32[384]{0:T(512)} %get-tuple-element.84) | copy-start | bytes 4612
  245.0 23.6 %copy-start.38 = (f32[2,1,256,256]{3,2,0,1:T(8,128)S(1)}, f32[2,1,256,256]{3,2,0,1:T(8,128)}, u32[]{:S(2)}) copy-start(f32[2,1,256,256]{3,2,0,1:T(8,128)} %copy.1523) | copy-start | bytes 1572868
  245.8 10.9 %all-to-all-start.7 = ((bf16[2,16,2,1,256]{4,2,0,3,1:T(2,128)(2,1)}), bf16[2,16,2,1,256]{4,2,0,3,1:T(2,128)(2,1)S(1)}, u32[]{:S(2)}, u32[]{:S(2)}) async-start(bf16[2,16,2,1,256]{4,2,0,3,1:T(2,128)(2,1)} %copy.1518), calls=%async_computation.7 | async-start | bytes 65536 | tf_op jit(solution)/shard_map/all_to_all | solution.py:207
  257.7 10.9 %all-to-all-start.8 = ((bf16[2,1,2,16,256]{4,2,0,1,3:T(2,128)(2,1)}), bf16[2,1,2,16,256]{4,2,0,1,3:T(2,128)(2,1)S(1)}, u32[]{:S(2)}, u32[]{:S(2)}) async-start(bf16[2,1,2,16,256]{4,2,0,1,3:T(2,128)(2,1)} %copy.1521), calls=%async_computation.8 | async-start | bytes 65536 | tf_op jit(solution)/shard_map/all_to_all | solution.py:196
  282.9 23.6 %copy-start.37 = (f32[2,1,256,256]{3,2,0,1:T(8,128)S(1)}, f32[2,1,256,256]{3,2,0,1:T(8,128)}, u32[]{:S(2)}) copy-start(f32[2,1,256,256]{3,2,0,1:T(8,128)} %copy.1533) | copy-start | bytes 1572868
  283.7 10.9 %all-to-all-start.9 = ((bf16[2,16,2,1,256]{4,2,0,3,1:T(2,128)(2,1)}), bf16[2,16,2,1,256]{4,2,0,3,1:T(2,128)(2,1)S(1)}, u32[]{:S(2)}, u32[]{:S(2)}) async-start(bf16[2,16,2,1,256]{4,2,0,3,1:T(2,128)(2,1)} %copy.1528), calls=%async_computation.9 | async-start | bytes 65536 | tf_op jit(solution)/shard_map/all_to_all | solution.py:207
  295.6 10.9 %all-to-all-start.10 = ((bf16[2,1,2,16,256]{4,2,0,1,3:T(2,128)(2,1)}), bf16[2,1,2,16,256]{4,2,0,1,3:T(2,128)(2,1)S(1)}, u32[]{:S(2)}, u32[]{:S(2)}) async-start(bf16[2,1,2,16,256]{4,2,0,1,3:T(2,128)(2,1)} %copy.1531), calls=%async_computation.10 | async-start | bytes 65536 | tf_op jit(solution)/shard_map/all_to_all | solution.py:196
  322.2 11.0 %all-to-all-start.11 = ((bf16[2,16,2,1,256]{4,2,0,3,1:T(2,128)(2,1)}), bf16[2,16,2,1,256]{4,2,0,3,1:T(2,128)(2,1)S(1)}, u32[]{:S(2)}, u32[]{:S(2)}) async-start(bf16[2,16,2,1,256]{4,2,0,3,1:T(2,128)(2,1)} %copy.1538), calls=%async_computation.11 | async-start | bytes 65536 | tf_op jit(solution)/shard_map/all_to_all | solution.py:207
  325.9 19.2 %copy-start.36 = (f32[2,1,256,256]{3,2,0,1:T(8,128)S(1)}, f32[2,1,256,256]{3,2,0,1:T(8,128)}, u32[]{:S(2)}) copy-start(f32[2,1,256,256]{3,2,0,1:T(8,128)} %copy.1543) | copy-start | bytes 1572868
  334.2 10.9 %all-to-all-start.12 = ((bf16[2,1,2,16,256]{4,2,0,1,3:T(2,128)(2,1)}), bf16[2,1,2,16,256]{4,2,0,1,3:T(2,128)(2,1)S(1)}, u32[]{:S(2)}, u32[]{:S(2)}) async-start(bf16[2,1,2,16,256]{4,2,0,1,3:T(2,128)(2,1)} %copy.1541), calls=%async_computation.12 | async-start | bytes 65536 | tf_op jit(solution)/shard_map/all_to_all | solution.py:196
  337.7 148.6 %all-reduce.4.cloned.1.call-start = ((), (), s32[]{:S(2)}) async-start(), calls=%async_computation.13 | async-start | bytes 2752512 | tf_op jit(solution)/shard_map/psum | solution.py:212
  357.6 136.5 %copy-start.74 = (f32[256,384]{1,0:T(8,128)S(1)}, f32[256,384]{1,0:T(8,128)}, u32[]{:S(2)}) copy-start(f32[256,384]{1,0:T(8,128)} %param.30) | copy-start | bytes 1179652
  486.4 7.7 %copy-start.73 = (f32[256,384]{1,0:T(8,128)S(1)}, f32[256,384]{1,0:T(8,128)}, u32[]{:S(2)}) copy-start(f32[256,384]{1,0:T(8,128)} %param.34) | copy-start | bytes 1179652
  488.1 6.0 %copy-start.40 = (f32[256,384]{1,0:T(8,128)S(1)}, f32[256,384]{1,0:T(8,128)}, u32[]{:S(2)}) copy-start(f32[256,384]{1,0:T(8,128)} %param.26) | copy-start | bytes 1179652
  (141 other events, 203.1 us)
Sparse Core Ops, SparseCore 0:
  357.0 129.3 all-reduce.3
